TPU v7x, 256 devices: a whole 4x4x8 slice. The times are simulated.
256 devices in a mesh: feat: 8 (over x, core), rows: 32 (over z, y).
Axes of the slice: x: 4, y: 4, z: 8, core: 2. Of those that a mesh axis runs over, the one named last changes fastest.
Arguments:
- features: bfloat16 [65536, 8192], P('rows', 'feat'), may hold values from -6 to 6
- residual: float32 [65536, 1024], P('rows', 'feat'), may hold values from -8 to 8
- inverse_grams: float32 [8192, 1024], P('feat'), may hold values from -1 to 1, as said below
Outputs:
- increments: bfloat16 [1024, 8192], P(None, 'feat')
- final_residual: float32 [65536, 1024], P('rows', 'feat')
Inputs may be any that keep to these rules, and one draw needn't show every extreme that they name: `inverse_grams`: each block of 1024 rows is a symmetric positive definite matrix.
All inputs are finite; a program needn't handle non-finite values.
Results may differ from a plain program's by a relative error of at most 0.0051.
Values may be sent and summed in bfloat16 or wider, within the bound.
A program may use at most 64 MiB of HBM per device.

v0:
```python
import jax
import jax.numpy as jnp
from jax import lax
from jax.sharding import PartitionSpec as P


def from_behind(value, axis, steps):
    count = lax.axis_size(axis)
    pairs = [(source, (source + steps) % count) for source in range(count)]
    return lax.ppermute(value, axis, pairs)


def on_device(features, residual, inverse_grams):
    block_total = lax.axis_size("feat")
    block_id = lax.axis_index("feat")
    piece_width = residual.shape[1]
    feat_width = features.shape[1]
    contract_rows = (((0,), (0,)), ((), ()))
    contract_cols = (((1,), (1,)), ((), ()))
    start_incr = jnp.zeros((piece_width * block_total, feat_width), jnp.bfloat16)

    def advance(visit, state_pair):
        current, increments = state_pair
        front_index = (block_id - visit) % block_total
        rounded = current.astype(jnp.bfloat16)
        partial_value = lax.dot_general(
            rounded, features, contract_rows, preferred_element_type=jnp.float32
        )
        summed_term = lax.psum(partial_value, "rows")
        update = lax.dot_general(
            summed_term, inverse_grams, contract_cols, precision=lax.Precision.HIGHEST
        ).astype(jnp.bfloat16)
        current = current - lax.dot_general(
            features, update, contract_cols, preferred_element_type=jnp.float32
        )
        increments = lax.dynamic_update_slice_in_dim(
            increments, update, front_index * piece_width, 0
        )
        current = from_behind(current, "feat", 1)
        return (current, increments)

    final_current, increments = lax.fori_loop(0, block_total, advance, (residual, start_incr))
    return (increments, final_current)


def solution(mesh):
    placed = (P("rows", "feat"), P("rows", "feat"), P("feat", None))
    return jax.shard_map(
        on_device,
        mesh=mesh,
        in_specs=placed,
        out_specs=(P(None, "feat"), P("rows", "feat")),
        check_vma=False,
    )
```

profile of v0, /device:TPU:1, one launch (start us, length us, event | category | flops | bytes accessed | tf_op | source)
XLA Modules:
  0.0 1415.4 jit_solution(5744996908963075979)
XLA Ops:
  10.3 1396.9 %while.17 = (s32[]{:T(128)}, f32[2048,128]{0,1:T(8,128)S(1)}, bf16[1024,1024]{1,0:T(8,128)(2,1)}, bf16[2048,1024]{1,0:T(8,128)(2,1)}, f32[1024,1024]{1,0:T(8,128...) while((s32[]{:T(128)}, f32[2048,128]{0,1:T(8,128)S(1)}, ...), condition=%wide.region_2.3_spmd, body=%wide.region_0.2_spmd.sunk | while | flops 2685140992 | bytes 41681292 | solution.py:42
  14.1 149.2 %all-reduce.2.cloned.1.call-done = f32[128,1024]{1,0:T(8,128)} async-done(((f32[128,1024]{1,0:T(8,128)}), f32[128,1024]{1,0:T(8,128)}) %all-reduce.2.cloned.1.call-update) | async-done | bytes 524304 | tf_op jit(solution)/shard_map/while/body/eval_jaxpr/psum | solution.py:29
  163.3 7.6 constant_dynamic-update-slice_fusion.2
  172.4 6.3 collective-permute-start
  178.7 11.7 collective-permute-done
  194.2 143.1 %all-reduce.2.cloned.1.call-done = f32[128,1024]{1,0:T(8,128)} async-done(((f32[128,1024]{1,0:T(8,128)}), f32[128,1024]{1,0:T(8,128)}) %all-reduce.2.cloned.1.call-update) | async-done | bytes 524304 | tf_op jit(solution)/shard_map/while/body/eval_jaxpr/psum | solution.py:29
  337.3 7.6 constant_dynamic-update-slice_fusion.2
  346.4 6.3 collective-permute-start
  352.6 11.7 collective-permute-done
  368.1 143.1 %all-reduce.2.cloned.1.call-done = f32[128,1024]{1,0:T(8,128)} async-done(((f32[128,1024]{1,0:T(8,128)}), f32[128,1024]{1,0:T(8,128)}) %all-reduce.2.cloned.1.call-update) | async-done | bytes 524304 | tf_op jit(solution)/shard_map/while/body/eval_jaxpr/psum | solution.py:29
  511.2 7.6 constant_dynamic-update-slice_fusion.2
  520.3 6.3 collective-permute-start
  526.6 11.7 collective-permute-done
  542.1 142.8 %all-reduce.2.cloned.1.call-done = f32[128,1024]{1,0:T(8,128)} async-done(((f32[128,1024]{1,0:T(8,128)}), f32[128,1024]{1,0:T(8,128)}) %all-reduce.2.cloned.1.call-update) | async-done | bytes 524304 | tf_op jit(solution)/shard_map/while/body/eval_jaxpr/psum | solution.py:29
  684.9 7.6 constant_dynamic-update-slice_fusion.2
  694.0 6.3 collective-permute-start
  700.2 11.7 collective-permute-done
  715.7 142.8 %all-reduce.2.cloned.1.call-done = f32[128,1024]{1,0:T(8,128)} async-done(((f32[128,1024]{1,0:T(8,128)}), f32[128,1024]{1,0:T(8,128)}) %all-reduce.2.cloned.1.call-update) | async-done | bytes 524304 | tf_op jit(solution)/shard_map/while/body/eval_jaxpr/psum | solution.py:29
  858.5 7.6 constant_dynamic-update-slice_fusion.2
  873.9 11.7 collective-permute-done
  889.4 142.8 %all-reduce.2.cloned.1.call-done = f32[128,1024]{1,0:T(8,128)} async-done(((f32[128,1024]{1,0:T(8,128)}), f32[128,1024]{1,0:T(8,128)}) %all-reduce.2.cloned.1.call-update) | async-done | bytes 524304 | tf_op jit(solution)/shard_map/while/body/eval_jaxpr/psum | solution.py:29
  1032.2 7.6 constant_dynamic-update-slice_fusion.2
  1041.3 6.3 collective-permute-start
  1047.6 11.7 collective-permute-done
  1063.1 143.1 %all-reduce.2.cloned.1.call-done = f32[128,1024]{1,0:T(8,128)} async-done(((f32[128,1024]{1,0:T(8,128)}), f32[128,1024]{1,0:T(8,128)}) %all-reduce.2.cloned.1.call-update) | async-done | bytes 524304 | tf_op jit(solution)/shard_map/while/body/eval_jaxpr/psum | solution.py:29
  1206.2 7.6 constant_dynamic-update-slice_fusion.2
  1215.3 6.3 collective-permute-start
  1221.5 11.7 collective-permute-done
  1237.0 143.1 %all-reduce.2.cloned.1.call-done = f32[128,1024]{1,0:T(8,128)} async-done(((f32[128,1024]{1,0:T(8,128)}), f32[128,1024]{1,0:T(8,128)}) %all-reduce.2.cloned.1.call-update) | async-done | bytes 524304 | tf_op jit(solution)/shard_map/while/body/eval_jaxpr/psum | solution.py:29
  1380.1 7.6 constant_dynamic-update-slice_fusion.2
  1389.3 6.3 collective-permute-start
  1395.5 11.7 collective-permute-done
  (52 shorter events, 52.7 us)
Async XLA Ops:
  10.3 153.0 %all-reduce.2.cloned.1.call-start = ((), (), s32[]{:S(2)}) async-start(), calls=%async_computation | async-start | bytes 1048576 | tf_op jit(solution)/shard_map/while/body/eval_jaxpr/psum | solution.py:29
  163.3 7.6 copy-start
  172.4 18.0 %collective-permute-start = (f32[2048,128]{0,1:T(8,128)S(1)}, f32[2048,128]{0,1:T(8,128)S(1)}, u32[]{:S(2)}, u32[]{:S(2)}) collective-permute-start(f32[2048,128]{0,1:T(8,128)S(1)} %fusion.23), channel_id=1, source_target_pairs={{0,32},{32,64},{64,96},{96,128},{128,160},{160,192},{192,224},{224... | collective-permute-start | bytes 3145736 | tf_op jit(solution)/shard_map/while/body/eval_jaxpr/ppermute | solution.py:10
  190.4 146.8 %all-reduce.2.cloned.1.call-start = ((), (), s32[]{:S(2)}) async-start(), calls=%async_computation | async-start | bytes 1048576 | tf_op jit(solution)/shard_map/while/body/eval_jaxpr/psum | solution.py:29
  337.3 7.6 copy-start
  346.4 18.0 %collective-permute-start = (f32[2048,128]{0,1:T(8,128)S(1)}, f32[2048,128]{0,1:T(8,128)S(1)}, u32[]{:S(2)}, u32[]{:S(2)}) collective-permute-start(f32[2048,128]{0,1:T(8,128)S(1)} %fusion.23), channel_id=1, source_target_pairs={{0,32},{32,64},{64,96},{96,128},{128,160},{160,192},{192,224},{224... | collective-permute-start | bytes 3145736 | tf_op jit(solution)/shard_map/while/body/eval_jaxpr/ppermute | solution.py:10
  364.4 146.8 %all-reduce.2.cloned.1.call-start = ((), (), s32[]{:S(2)}) async-start(), calls=%async_computation | async-start | bytes 1048576 | tf_op jit(solution)/shard_map/while/body/eval_jaxpr/psum | solution.py:29
  511.2 7.6 copy-start
  520.3 18.0 %collective-permute-start = (f32[2048,128]{0,1:T(8,128)S(1)}, f32[2048,128]{0,1:T(8,128)S(1)}, u32[]{:S(2)}, u32[]{:S(2)}) collective-permute-start(f32[2048,128]{0,1:T(8,128)S(1)} %fusion.23), channel_id=1, source_target_pairs={{0,32},{32,64},{64,96},{96,128},{128,160},{160,192},{192,224},{224... | collective-permute-start | bytes 3145736 | tf_op jit(solution)/shard_map/while/body/eval_jaxpr/ppermute | solution.py:10
  538.3 146.5 %all-reduce.2.cloned.1.call-start = ((), (), s32[]{:S(2)}) async-start(), calls=%async_computation | async-start | bytes 1048576 | tf_op jit(solution)/shard_map/while/body/eval_jaxpr/psum | solution.py:29
  684.9 7.6 copy-start
  694.0 18.0 %collective-permute-start = (f32[2048,128]{0,1:T(8,128)S(1)}, f32[2048,128]{0,1:T(8,128)S(1)}, u32[]{:S(2)}, u32[]{:S(2)}) collective-permute-start(f32[2048,128]{0,1:T(8,128)S(1)} %fusion.23), channel_id=1, source_target_pairs={{0,32},{32,64},{64,96},{96,128},{128,160},{160,192},{192,224},{224... | collective-permute-start | bytes 3145736 | tf_op jit(solution)/shard_map/while/body/eval_jaxpr/ppermute | solution.py:10
  712.0 146.5 %all-reduce.2.cloned.1.call-start = ((), (), s32[]{:S(2)}) async-start(), calls=%async_computation | async-start | bytes 1048576 | tf_op jit(solution)/shard_map/while/body/eval_jaxpr/psum | solution.py:29
  858.5 7.6 copy-start
  867.6 18.0 %collective-permute-start = (f32[2048,128]{0,1:T(8,128)S(1)}, f32[2048,128]{0,1:T(8,128)S(1)}, u32[]{:S(2)}, u32[]{:S(2)}) collective-permute-start(f32[2048,128]{0,1:T(8,128)S(1)} %fusion.23), channel_id=1, source_target_pairs={{0,32},{32,64},{64,96},{96,128},{128,160},{160,192},{192,224},{224... | collective-permute-start | bytes 3145736 | tf_op jit(solution)/shard_map/while/body/eval_jaxpr/ppermute | solution.py:10
  885.6 146.5 %all-reduce.2.cloned.1.call-start = ((), (), s32[]{:S(2)}) async-start(), calls=%async_computation | async-start | bytes 1048576 | tf_op jit(solution)/shard_map/while/body/eval_jaxpr/psum | solution.py:29
  1032.2 7.6 copy-start
  1041.3 18.0 %collective-permute-start = (f32[2048,128]{0,1:T(8,128)S(1)}, f32[2048,128]{0,1:T(8,128)S(1)}, u32[]{:S(2)}, u32[]{:S(2)}) collective-permute-start(f32[2048,128]{0,1:T(8,128)S(1)} %fusion.23), channel_id=1, source_target_pairs={{0,32},{32,64},{64,96},{96,128},{128,160},{160,192},{192,224},{224... | collective-permute-start | bytes 3145736 | tf_op jit(solution)/shard_map/while/body/eval_jaxpr/ppermute | solution.py:10
  1059.3 146.8 %all-reduce.2.cloned.1.call-start = ((), (), s32[]{:S(2)}) async-start(), calls=%async_computation | async-start | bytes 1048576 | tf_op jit(solution)/shard_map/while/body/eval_jaxpr/psum | solution.py:29
  1206.2 7.6 copy-start
  1215.3 18.0 %collective-permute-start = (f32[2048,128]{0,1:T(8,128)S(1)}, f32[2048,128]{0,1:T(8,128)S(1)}, u32[]{:S(2)}, u32[]{:S(2)}) collective-permute-start(f32[2048,128]{0,1:T(8,128)S(1)} %fusion.23), channel_id=1, source_target_pairs={{0,32},{32,64},{64,96},{96,128},{128,160},{160,192},{192,224},{224... | collective-permute-start | bytes 3145736 | tf_op jit(solution)/shard_map/while/body/eval_jaxpr/ppermute | solution.py:10
  1233.3 146.8 %all-reduce.2.cloned.1.call-start = ((), (), s32[]{:S(2)}) async-start(), calls=%async_computation | async-start | bytes 1048576 | tf_op jit(solution)/shard_map/while/body/eval_jaxpr/psum | solution.py:29
  1380.1 7.6 copy-start
  1389.3 18.0 %collective-permute-start = (f32[2048,128]{0,1:T(8,128)S(1)}, f32[2048,128]{0,1:T(8,128)S(1)}, u32[]{:S(2)}, u32[]{:S(2)}) collective-permute-start(f32[2048,128]{0,1:T(8,128)S(1)} %fusion.23), channel_id=1, source_target_pairs={{0,32},{32,64},{64,96},{96,128},{128,160},{160,192},{192,224},{224... | collective-permute-start | bytes 3145736 | tf_op jit(solution)/shard_map/while/body/eval_jaxpr/ppermute | solution.py:10
Sparse Core Ops, SparseCore 0:
  15.1 148.1 all-reduce.1
  195.2 142.0 all-reduce.1
  369.2 141.9 all-reduce.1
  542.8 142.0 all-reduce.1
  716.4 142.0 all-reduce.1
  890.1 142.0 all-reduce.1
  1064.1 142.0 all-reduce.1
  1238.1 142.0 all-reduce.1
where the time goes:
time: 1420 us
  waiting for transfers between devices  1240 us (87%)
  matrix products  102 us (7%)
  starting transfers between devices  50.1 us (4%)
    psum x8, waiting for transfers between devices, advance(): summed_term = lax.psum(partial_value, 'rows')  1150 us
    ppermute x8, waiting for transfers between devices, from_behind(): return lax.ppermute(value, axis, pairs)  93.9 us
    dot_general x8, matrix products, advance(): lax.dot_general(summed_term, inverse_grams, contract_cols, precision=lax....  60.7 us
    ppermute x8, starting transfers between devices, from_behind(): return lax.ppermute(value, axis, pairs)  50.1 us
    dot_general x8, matrix products, advance(): lax.dot_general(rounded, features, contract_rows, preferred_element_type=...  29.6 us
  transfers between devices with their start and end apart: 16, of which 16 were waited for; matrix products, arithmetic and copies ran while one was open for 0% of the time, Pallas kernels for 0%

commit v1 on v0

--- a/solution.py
+++ b/solution.py
@@ -26,7 +26,11 @@
         partial_value = lax.dot_general(
             rounded, features, contract_rows, preferred_element_type=jnp.float32
         )
-        summed_term = lax.psum(partial_value, "rows")
+        summed_term = partial_value
+        for hop in (1, 2, 4, 8, 16):
+            summed_term = summed_term + lax.ppermute(
+                summed_term, "rows", [(dev, dev ^ hop) for dev in range(32)]
+            )
         update = lax.dot_general(
             summed_term, inverse_grams, contract_cols, precision=lax.Precision.HIGHEST
         ).astype(jnp.bfloat16)

time: 1420 us -> 960 us (0.68)
  waiting for transfers between devices: 1240 us -> 691 us
  starting transfers between devices: 50.1 us -> 154 us
    psum x8 -> x0, waiting for transfers between devices: 1150 us -> none  [advance(): summed_term = lax.psum(partial_value, 'rows')]
    ppermute x0 -> x40, waiting for transfers between devices: none -> 597 us  [advance(): lax.ppermute(summed_term, 'rows', [(dev, dev ^ hop) for dev in range(32)])]
    ppermute x0 -> x40, starting transfers between devices: none -> 77.9 us  [advance(): lax.ppermute(summed_term, 'rows', [(dev, dev ^ hop) for dev in range(32)])]
    ppermute x8, starting transfers between devices: 50.1 us -> 75.7 us  [from_behind(): return lax.ppermute(value, axis, pairs)]
  transfers between devices with their start and end apart: 16 -> 48, of which waited for: 16 -> 48; matrix products, arithmetic and copies ran while one was open for 0% -> 0% of each run, Pallas kernels for 0% -> 0%
where the time goes in v1:
time: 960 us; the launch traced here: 945 us
  waiting for transfers between devices  691 us (72%)
  starting transfers between devices  154 us (16%)
  matrix products  93.2 us (10%)
    ppermute x40, waiting for transfers between devices, advance(): lax.ppermute(summed_term, 'rows', [(dev, dev ^ hop) for dev in range(32)])  597 us
    ppermute x8, waiting for transfers between devices, from_behind(): return lax.ppermute(value, axis, pairs)  93.9 us
    ppermute x40, starting transfers between devices, advance(): lax.ppermute(summed_term, 'rows', [(dev, dev ^ hop) for dev in range(32)])  77.9 us
    ppermute x8, starting transfers between devices, from_behind(): return lax.ppermute(value, axis, pairs)  75.7 us
    dot_general x8, matrix products, advance(): lax.dot_general(summed_term, inverse_grams, contract_cols, precision=lax....  57.8 us
    dot_general x8, matrix products, advance(): lax.dot_general(rounded, features, contract_rows, preferred_element_type=...  23.2 us
  transfers between devices with their start and end apart: 48, of which 48 were waited for; matrix products, arithmetic and copies ran while one was open for 0% of the time, Pallas kernels for 0%

profile of v1, /device:TPU:1, one launch (start us, length us, event | category | flops | bytes accessed | tf_op | source)
XLA Modules:
  0.0 945.0 jit_solution(1106211221373536959)
XLA Ops:
  3.8 940.0 %while.17 = (s32[]{:T(128)}, f32[2048,128]{0,1:T(8,128)S(1)}, bf16[1024,1024]{1,0:T(8,128)(2,1)}, bf16[2048,1024]{1,0:T(8,128)(2,1)}, f32[1024,1024]{1,0:T(8,128...) while((s32[]{:T(128)}, f32[2048,128]{0,1:T(8,128)S(1)}, ...), condition=%wide.region_1.2_spmd, body=%wide.region_0.1_spmd.sunk | while | flops 2685665280 | bytes 55837228 | solution.py:46
  48.8 22.6 %collective-permute-done.3 = f32[128,1024]{1,0:T(8,128)S(1)} collective-permute-done((f32[128,1024]{1,0:T(8,128)S(1)}, f32[128,1024]{1,0:T(8,128)S(1)}, u32[]{:S(2)}, u32[]{:S(2)}) %collective-permute-start.3) | collective-permute-done | bytes 524320 | tf_op jit(solution)/shard_map/while/body/eval_jaxpr/ppermute | solution.py:31
  78.0 22.7 %collective-permute-done.4 = f32[128,1024]{1,0:T(8,128)S(1)} collective-permute-done((f32[128,1024]{1,0:T(8,128)S(1)}, f32[128,1024]{1,0:T(8,128)S(1)}, u32[]{:S(2)}, u32[]{:S(2)}) %collective-permute-start.4) | collective-permute-done | bytes 524320 | tf_op jit(solution)/shard_map/while/body/eval_jaxpr/ppermute | solution.py:31
  112.1 11.7 %collective-permute-done.5 = f32[2048,128]{0,1:T(8,128)S(1)} collective-permute-done((f32[2048,128]{0,1:T(8,128)S(1)}, f32[2048,128]{0,1:T(8,128)S(1)}, u32[]{:S(2)}, u32[]{:S(2)}) %collective-permute-start.5) | collective-permute-done | bytes 1048608 | tf_op jit(solution)/shard_map/while/body/eval_jaxpr/ppermute | solution.py:10
  164.6 22.2 %collective-permute-done.3 = f32[128,1024]{1,0:T(8,128)S(1)} collective-permute-done((f32[128,1024]{1,0:T(8,128)S(1)}, f32[128,1024]{1,0:T(8,128)S(1)}, u32[]{:S(2)}, u32[]{:S(2)}) %collective-permute-start.3) | collective-permute-done | bytes 524320 | tf_op jit(solution)/shard_map/while/body/eval_jaxpr/ppermute | solution.py:31
  190.5 25.0 %collective-permute-done.4 = f32[128,1024]{1,0:T(8,128)S(1)} collective-permute-done((f32[128,1024]{1,0:T(8,128)S(1)}, f32[128,1024]{1,0:T(8,128)S(1)}, u32[]{:S(2)}, u32[]{:S(2)}) %collective-permute-start.4) | collective-permute-done | bytes 524320 | tf_op jit(solution)/shard_map/while/body/eval_jaxpr/ppermute | solution.py:31
  227.0 11.7 %collective-permute-done.5 = f32[2048,128]{0,1:T(8,128)S(1)} collective-permute-done((f32[2048,128]{0,1:T(8,128)S(1)}, f32[2048,128]{0,1:T(8,128)S(1)}, u32[]{:S(2)}, u32[]{:S(2)}) %collective-permute-start.5) | collective-permute-done | bytes 1048608 | tf_op jit(solution)/shard_map/while/body/eval_jaxpr/ppermute | solution.py:10
  256.2 11.5 %collective-permute-done.1 = f32[128,1024]{1,0:T(8,128)S(1)} collective-permute-done((f32[128,1024]{1,0:T(8,128)S(1)}, f32[128,1024]{1,0:T(8,128)S(1)}, u32[]{:S(2)}, u32[]{:S(2)}) %collective-permute-start.1) | collective-permute-done | bytes 524320 | tf_op jit(solution)/shard_map/while/body/eval_jaxpr/ppermute | solution.py:31
  283.6 22.7 %collective-permute-done.3 = f32[128,1024]{1,0:T(8,128)S(1)} collective-permute-done((f32[128,1024]{1,0:T(8,128)S(1)}, f32[128,1024]{1,0:T(8,128)S(1)}, u32[]{:S(2)}, u32[]{:S(2)}) %collective-permute-start.3) | collective-permute-done | bytes 524320 | tf_op jit(solution)/shard_map/while/body/eval_jaxpr/ppermute | solution.py:31
  309.5 25.9 %collective-permute-done.4 = f32[128,1024]{1,0:T(8,128)S(1)} collective-permute-done((f32[128,1024]{1,0:T(8,128)S(1)}, f32[128,1024]{1,0:T(8,128)S(1)}, u32[]{:S(2)}, u32[]{:S(2)}) %collective-permute-start.4) | collective-permute-done | bytes 524320 | tf_op jit(solution)/shard_map/while/body/eval_jaxpr/ppermute | solution.py:31
  344.2 11.7 %collective-permute-done.5 = f32[2048,128]{0,1:T(8,128)S(1)} collective-permute-done((f32[2048,128]{0,1:T(8,128)S(1)}, f32[2048,128]{0,1:T(8,128)S(1)}, u32[]{:S(2)}, u32[]{:S(2)}) %collective-permute-start.5) | collective-permute-done | bytes 1048608 | tf_op jit(solution)/shard_map/while/body/eval_jaxpr/ppermute | solution.py:10
  406.1 19.7 %collective-permute-done.4 = f32[128,1024]{1,0:T(8,128)S(1)} collective-permute-done((f32[128,1024]{1,0:T(8,128)S(1)}, f32[128,1024]{1,0:T(8,128)S(1)}, u32[]{:S(2)}, u32[]{:S(2)}) %collective-permute-start.4) | collective-permute-done | bytes 524320 | tf_op jit(solution)/shard_map/while/body/eval_jaxpr/ppermute | solution.py:31
  434.6 19.7 %collective-permute-start.5 = (f32[2048,128]{0,1:T(8,128)S(1)}, f32[2048,128]{0,1:T(8,128)S(1)}, u32[]{:S(2)}, u32[]{:S(2)}) collective-permute-start(f32[2048,128]{0,1:T(8,128)S(1)} %fusion.21), channel_id=1, source_target_pairs={{0,32},{32,64},{64,96},{96,128},{128,160},{160,192},{192,224},{224... | collective-permute-start | bytes 3145736 | tf_op jit(solution)/shard_map/while/body/eval_jaxpr/ppermute | solution.py:10
  454.3 11.7 %collective-permute-done.5 = f32[2048,128]{0,1:T(8,128)S(1)} collective-permute-done((f32[2048,128]{0,1:T(8,128)S(1)}, f32[2048,128]{0,1:T(8,128)S(1)}, u32[]{:S(2)}, u32[]{:S(2)}) %collective-permute-start.5) | collective-permute-done | bytes 1048608 | tf_op jit(solution)/shard_map/while/body/eval_jaxpr/ppermute | solution.py:10
  479.0 12.5 %collective-permute-done.1 = f32[128,1024]{1,0:T(8,128)S(1)} collective-permute-done((f32[128,1024]{1,0:T(8,128)S(1)}, f32[128,1024]{1,0:T(8,128)S(1)}, u32[]{:S(2)}, u32[]{:S(2)}) %collective-permute-start.1) | collective-permute-done | bytes 524320 | tf_op jit(solution)/shard_map/while/body/eval_jaxpr/ppermute | solution.py:31
  502.2 12.6 %collective-permute-done.3 = f32[128,1024]{1,0:T(8,128)S(1)} collective-permute-done((f32[128,1024]{1,0:T(8,128)S(1)}, f32[128,1024]{1,0:T(8,128)S(1)}, u32[]{:S(2)}, u32[]{:S(2)}) %collective-permute-start.3) | collective-permute-done | bytes 524320 | tf_op jit(solution)/shard_map/while/body/eval_jaxpr/ppermute | solution.py:31
  517.7 19.5 %collective-permute-done.4 = f32[128,1024]{1,0:T(8,128)S(1)} collective-permute-done((f32[128,1024]{1,0:T(8,128)S(1)}, f32[128,1024]{1,0:T(8,128)S(1)}, u32[]{:S(2)}, u32[]{:S(2)}) %collective-permute-start.4) | collective-permute-done | bytes 524320 | tf_op jit(solution)/shard_map/while/body/eval_jaxpr/ppermute | solution.py:31
  546.0 29.5 %collective-permute-start.5 = (f32[2048,128]{0,1:T(8,128)S(1)}, f32[2048,128]{0,1:T(8,128)S(1)}, u32[]{:S(2)}, u32[]{:S(2)}) collective-permute-start(f32[2048,128]{0,1:T(8,128)S(1)} %fusion.21), channel_id=1, source_target_pairs={{0,32},{32,64},{64,96},{96,128},{128,160},{160,192},{192,224},{224... | collective-permute-start | bytes 3145736 | tf_op jit(solution)/shard_map/while/body/eval_jaxpr/ppermute | solution.py:10
  575.5 11.7 %collective-permute-done.5 = f32[2048,128]{0,1:T(8,128)S(1)} collective-permute-done((f32[2048,128]{0,1:T(8,128)S(1)}, f32[2048,128]{0,1:T(8,128)S(1)}, u32[]{:S(2)}, u32[]{:S(2)}) %collective-permute-start.5) | collective-permute-done | bytes 1048608 | tf_op jit(solution)/shard_map/while/body/eval_jaxpr/ppermute | solution.py:10
  591.5 12.7 %collective-permute-done = f32[128,1024]{1,0:T(8,128)S(1)} collective-permute-done((f32[128,1024]{1,0:T(8,128)S(1)}, f32[128,1024]{1,0:T(8,128)S(1)}, u32[]{:S(2)}, u32[]{:S(2)}) %collective-permute-start) | collective-permute-done | bytes 524320 | tf_op jit(solution)/shard_map/while/body/eval_jaxpr/ppermute | solution.py:31
  604.3 14.6 %collective-permute-done.1 = f32[128,1024]{1,0:T(8,128)S(1)} collective-permute-done((f32[128,1024]{1,0:T(8,128)S(1)}, f32[128,1024]{1,0:T(8,128)S(1)}, u32[]{:S(2)}, u32[]{:S(2)}) %collective-permute-start.1) | collective-permute-done | bytes 524320 | tf_op jit(solution)/shard_map/while/body/eval_jaxpr/ppermute | solution.py:31
  619.1 12.2 %collective-permute-done.2 = f32[128,1024]{1,0:T(8,128)S(1)} collective-permute-done((f32[128,1024]{1,0:T(8,128)S(1)}, f32[128,1024]{1,0:T(8,128)S(1)}, u32[]{:S(2)}, u32[]{:S(2)}) %collective-permute-start.2) | collective-permute-done | bytes 524320 | tf_op jit(solution)/shard_map/while/body/eval_jaxpr/ppermute | solution.py:31
  633.5 23.4 %collective-permute-done.3 = f32[128,1024]{1,0:T(8,128)S(1)} collective-permute-done((f32[128,1024]{1,0:T(8,128)S(1)}, f32[128,1024]{1,0:T(8,128)S(1)}, u32[]{:S(2)}, u32[]{:S(2)}) %collective-permute-start.3) | collective-permute-done | bytes 524320 | tf_op jit(solution)/shard_map/while/body/eval_jaxpr/ppermute | solution.py:31
  659.9 25.9 %collective-permute-done.4 = f32[128,1024]{1,0:T(8,128)S(1)} collective-permute-done((f32[128,1024]{1,0:T(8,128)S(1)}, f32[128,1024]{1,0:T(8,128)S(1)}, u32[]{:S(2)}, u32[]{:S(2)}) %collective-permute-start.4) | collective-permute-done | bytes 524320 | tf_op jit(solution)/shard_map/while/body/eval_jaxpr/ppermute | solution.py:31
  694.5 11.7 %collective-permute-done.5 = f32[2048,128]{0,1:T(8,128)S(1)} collective-permute-done((f32[2048,128]{0,1:T(8,128)S(1)}, f32[2048,128]{0,1:T(8,128)S(1)}, u32[]{:S(2)}, u32[]{:S(2)}) %collective-permute-start.5) | collective-permute-done | bytes 1048608 | tf_op jit(solution)/shard_map/while/body/eval_jaxpr/ppermute | solution.py:10
  744.4 48.6 %collective-permute-done.3 = f32[128,1024]{1,0:T(8,128)S(1)} collective-permute-done((f32[128,1024]{1,0:T(8,128)S(1)}, f32[128,1024]{1,0:T(8,128)S(1)}, u32[]{:S(2)}, u32[]{:S(2)}) %collective-permute-start.3) | collective-permute-done | bytes 524320 | tf_op jit(solution)/shard_map/while/body/eval_jaxpr/ppermute | solution.py:31
  793.2 25.3 %collective-permute-done.4 = f32[128,1024]{1,0:T(8,128)S(1)} collective-permute-done((f32[128,1024]{1,0:T(8,128)S(1)}, f32[128,1024]{1,0:T(8,128)S(1)}, u32[]{:S(2)}, u32[]{:S(2)}) %collective-permute-start.4) | collective-permute-done | bytes 524320 | tf_op jit(solution)/shard_map/while/body/eval_jaxpr/ppermute | solution.py:31
  827.3 11.7 %collective-permute-done.5 = f32[2048,128]{0,1:T(8,128)S(1)} collective-permute-done((f32[2048,128]{0,1:T(8,128)S(1)}, f32[2048,128]{0,1:T(8,128)S(1)}, u32[]{:S(2)}, u32[]{:S(2)}) %collective-permute-start.5) | collective-permute-done | bytes 1048608 | tf_op jit(solution)/shard_map/while/body/eval_jaxpr/ppermute | solution.py:10
  870.6 14.9 %collective-permute-done.3 = f32[128,1024]{1,0:T(8,128)S(1)} collective-permute-done((f32[128,1024]{1,0:T(8,128)S(1)}, f32[128,1024]{1,0:T(8,128)S(1)}, u32[]{:S(2)}, u32[]{:S(2)}) %collective-permute-start.3) | collective-permute-done | bytes 524320 | tf_op jit(solution)/shard_map/while/body/eval_jaxpr/ppermute | solution.py:31
  889.2 13.0 %collective-permute-done.4 = f32[128,1024]{1,0:T(8,128)S(1)} collective-permute-done((f32[128,1024]{1,0:T(8,128)S(1)}, f32[128,1024]{1,0:T(8,128)S(1)}, u32[]{:S(2)}, u32[]{:S(2)}) %collective-permute-start.4) | collective-permute-done | bytes 524320 | tf_op jit(solution)/shard_map/while/body/eval_jaxpr/ppermute | solution.py:31
  911.0 21.0 %collective-permute-start.5 = (f32[2048,128]{0,1:T(8,128)S(1)}, f32[2048,128]{0,1:T(8,128)S(1)}, u32[]{:S(2)}, u32[]{:S(2)}) collective-permute-start(f32[2048,128]{0,1:T(8,128)S(1)} %fusion.21), channel_id=1, source_target_pairs={{0,32},{32,64},{64,96},{96,128},{128,160},{160,192},{192,224},{224... | collective-permute-start | bytes 3145736 | tf_op jit(solution)/shard_map/while/body/eval_jaxpr/ppermute | solution.py:10
  932.0 11.7 %collective-permute-done.5 = f32[2048,128]{0,1:T(8,128)S(1)} collective-permute-done((f32[2048,128]{0,1:T(8,128)S(1)}, f32[2048,128]{0,1:T(8,128)S(1)}, u32[]{:S(2)}, u32[]{:S(2)}) %collective-permute-start.5) | collective-permute-done | bytes 1048608 | tf_op jit(solution)/shard_map/while/body/eval_jaxpr/ppermute | solution.py:10
  (140 shorter events, 372.3 us)
Async XLA Ops:
  6.7 12.7 %collective-permute-start = (f32[128,1024]{1,0:T(8,128)S(1)}, f32[128,1024]{1,0:T(8,128)S(1)}, u32[]{:S(2)}, u32[]{:S(2)}) collective-permute-start(f32[128,1024]{1,0:T(8,128)S(1)} %fusion.20), channel_id=1, source_target_pairs={{0,1},{1,0},{2,3},{3,2},{4,5},{5,4},{6,7},{7,6},{8,9},{9,8},{10,11... | collective-permute-start | bytes 1572872 | tf_op jit(solution)/shard_map/while/body/eval_jaxpr/ppermute | solution.py:31
  19.4 14.6 %collective-permute-start.1 = (f32[128,1024]{1,0:T(8,128)S(1)}, f32[128,1024]{1,0:T(8,128)S(1)}, u32[]{:S(2)}, u32[]{:S(2)}) collective-permute-start(f32[128,1024]{1,0:T(8,128)S(1)} %add.107), channel_id=1, source_target_pairs={{0,2},{1,3},{2,0},{3,1},{4,6},{5,7},{6,4},{7,5},{8,10},{9,11},{10,... | collective-permute-start | bytes 1572872 | tf_op jit(solution)/shard_map/while/body/eval_jaxpr/ppermute | solution.py:31
  45.7 25.7 %collective-permute-start.3 = (f32[128,1024]{1,0:T(8,128)S(1)}, f32[128,1024]{1,0:T(8,128)S(1)}, u32[]{:S(2)}, u32[]{:S(2)}) collective-permute-start(f32[128,1024]{1,0:T(8,128)S(1)} %add.109), channel_id=1, source_target_pairs={{0,8},{1,9},{2,10},{3,11},{4,12},{5,13},{6,14},{7,15},{8,0},{9,1},... | collective-permute-start | bytes 1572872 | tf_op jit(solution)/shard_map/while/body/eval_jaxpr/ppermute | solution.py:31
  71.5 29.2 %collective-permute-start.4 = (f32[128,1024]{1,0:T(8,128)S(1)}, f32[128,1024]{1,0:T(8,128)S(1)}, u32[]{:S(2)}, u32[]{:S(2)}) collective-permute-start(f32[128,1024]{1,0:T(8,128)S(1)} %add.110), channel_id=1, source_target_pairs={{0,16},{1,17},{2,18},{3,19},{4,20},{5,21},{6,22},{7,23},{8,24},{9,... | collective-permute-start | bytes 1572872 | tf_op jit(solution)/shard_map/while/body/eval_jaxpr/ppermute | solution.py:31
  109.4 14.4 %collective-permute-start.5 = (f32[2048,128]{0,1:T(8,128)S(1)}, f32[2048,128]{0,1:T(8,128)S(1)}, u32[]{:S(2)}, u32[]{:S(2)}) collective-permute-start(f32[2048,128]{0,1:T(8,128)S(1)} %fusion.21), channel_id=1, source_target_pairs={{0,32},{32,64},{64,96},{96,128},{128,160},{160,192},{192,224},{224... | collective-permute-start | bytes 3145736 | tf_op jit(solution)/shard_map/while/body/eval_jaxpr/ppermute | solution.py:10
  137.8 13.9 %collective-permute-start.1 = (f32[128,1024]{1,0:T(8,128)S(1)}, f32[128,1024]{1,0:T(8,128)S(1)}, u32[]{:S(2)}, u32[]{:S(2)}) collective-permute-start(f32[128,1024]{1,0:T(8,128)S(1)} %add.107), channel_id=1, source_target_pairs={{0,2},{1,3},{2,0},{3,1},{4,6},{5,7},{6,4},{7,5},{8,10},{9,11},{10,... | collective-permute-start | bytes 1572872 | tf_op jit(solution)/shard_map/while/body/eval_jaxpr/ppermute | solution.py:31
  162.2 24.6 %collective-permute-start.3 = (f32[128,1024]{1,0:T(8,128)S(1)}, f32[128,1024]{1,0:T(8,128)S(1)}, u32[]{:S(2)}, u32[]{:S(2)}) collective-permute-start(f32[128,1024]{1,0:T(8,128)S(1)} %add.109), channel_id=1, source_target_pairs={{0,8},{1,9},{2,10},{3,11},{4,12},{5,13},{6,14},{7,15},{8,0},{9,1},... | collective-permute-start | bytes 1572872 | tf_op jit(solution)/shard_map/while/body/eval_jaxpr/ppermute | solution.py:31
  186.9 28.6 %collective-permute-start.4 = (f32[128,1024]{1,0:T(8,128)S(1)}, f32[128,1024]{1,0:T(8,128)S(1)}, u32[]{:S(2)}, u32[]{:S(2)}) collective-permute-start(f32[128,1024]{1,0:T(8,128)S(1)} %add.110), channel_id=1, source_target_pairs={{0,16},{1,17},{2,18},{3,19},{4,20},{5,21},{6,22},{7,23},{8,24},{9,... | collective-permute-start | bytes 1572872 | tf_op jit(solution)/shard_map/while/body/eval_jaxpr/ppermute | solution.py:31
  224.3 14.5 %collective-permute-start.5 = (f32[2048,128]{0,1:T(8,128)S(1)}, f32[2048,128]{0,1:T(8,128)S(1)}, u32[]{:S(2)}, u32[]{:S(2)}) collective-permute-start(f32[2048,128]{0,1:T(8,128)S(1)} %fusion.21), channel_id=1, source_target_pairs={{0,32},{32,64},{64,96},{96,128},{128,160},{160,192},{192,224},{224... | collective-permute-start | bytes 3145736 | tf_op jit(solution)/shard_map/while/body/eval_jaxpr/ppermute | solution.py:10
  253.8 13.9 %collective-permute-start.1 = (f32[128,1024]{1,0:T(8,128)S(1)}, f32[128,1024]{1,0:T(8,128)S(1)}, u32[]{:S(2)}, u32[]{:S(2)}) collective-permute-start(f32[128,1024]{1,0:T(8,128)S(1)} %add.107), channel_id=1, source_target_pairs={{0,2},{1,3},{2,0},{3,1},{4,6},{5,7},{6,4},{7,5},{8,10},{9,11},{10,... | collective-permute-start | bytes 1572872 | tf_op jit(solution)/shard_map/while/body/eval_jaxpr/ppermute | solution.py:31
  279.3 27.1 %collective-permute-start.3 = (f32[128,1024]{1,0:T(8,128)S(1)}, f32[128,1024]{1,0:T(8,128)S(1)}, u32[]{:S(2)}, u32[]{:S(2)}) collective-permute-start(f32[128,1024]{1,0:T(8,128)S(1)} %add.109), channel_id=1, source_target_pairs={{0,8},{1,9},{2,10},{3,11},{4,12},{5,13},{6,14},{7,15},{8,0},{9,1},... | collective-permute-start | bytes 1572872 | tf_op jit(solution)/shard_map/while/body/eval_jaxpr/ppermute | solution.py:31
  306.4 29.0 %collective-permute-start.4 = (f32[128,1024]{1,0:T(8,128)S(1)}, f32[128,1024]{1,0:T(8,128)S(1)}, u32[]{:S(2)}, u32[]{:S(2)}) collective-permute-start(f32[128,1024]{1,0:T(8,128)S(1)} %add.110), channel_id=1, source_target_pairs={{0,16},{1,17},{2,18},{3,19},{4,20},{5,21},{6,22},{7,23},{8,24},{9,... | collective-permute-start | bytes 1572872 | tf_op jit(solution)/shard_map/while/body/eval_jaxpr/ppermute | solution.py:31
  368.3 12.9 %collective-permute-start.1 = (f32[128,1024]{1,0:T(8,128)S(1)}, f32[128,1024]{1,0:T(8,128)S(1)}, u32[]{:S(2)}, u32[]{:S(2)}) collective-permute-start(f32[128,1024]{1,0:T(8,128)S(1)} %add.107), channel_id=1, source_target_pairs={{0,2},{1,3},{2,0},{3,1},{4,6},{5,7},{6,4},{7,5},{8,10},{9,11},{10,... | collective-permute-start | bytes 1572872 | tf_op jit(solution)/shard_map/while/body/eval_jaxpr/ppermute | solution.py:31
  389.4 14.2 %collective-permute-start.3 = (f32[128,1024]{1,0:T(8,128)S(1)}, f32[128,1024]{1,0:T(8,128)S(1)}, u32[]{:S(2)}, u32[]{:S(2)}) collective-permute-start(f32[128,1024]{1,0:T(8,128)S(1)} %add.109), channel_id=1, source_target_pairs={{0,8},{1,9},{2,10},{3,11},{4,12},{5,13},{6,14},{7,15},{8,0},{9,1},... | collective-permute-start | bytes 1572872 | tf_op jit(solution)/shard_map/while/body/eval_jaxpr/ppermute | solution.py:31
  403.7 22.2 %collective-permute-start.4 = (f32[128,1024]{1,0:T(8,128)S(1)}, f32[128,1024]{1,0:T(8,128)S(1)}, u32[]{:S(2)}, u32[]{:S(2)}) collective-permute-start(f32[128,1024]{1,0:T(8,128)S(1)} %add.110), channel_id=1, source_target_pairs={{0,16},{1,17},{2,18},{3,19},{4,20},{5,21},{6,22},{7,23},{8,24},{9,... | collective-permute-start | bytes 1572872 | tf_op jit(solution)/shard_map/while/body/eval_jaxpr/ppermute | solution.py:31
  434.6 31.4 %collective-permute-start.5 = (f32[2048,128]{0,1:T(8,128)S(1)}, f32[2048,128]{0,1:T(8,128)S(1)}, u32[]{:S(2)}, u32[]{:S(2)}) collective-permute-start(f32[2048,128]{0,1:T(8,128)S(1)} %fusion.21), channel_id=1, source_target_pairs={{0,32},{32,64},{64,96},{96,128},{128,160},{160,192},{192,224},{224... | collective-permute-start | bytes 3145736 | tf_op jit(solution)/shard_map/while/body/eval_jaxpr/ppermute | solution.py:10
  477.1 14.4 %collective-permute-start.1 = (f32[128,1024]{1,0:T(8,128)S(1)}, f32[128,1024]{1,0:T(8,128)S(1)}, u32[]{:S(2)}, u32[]{:S(2)}) collective-permute-start(f32[128,1024]{1,0:T(8,128)S(1)} %add.107), channel_id=1, source_target_pairs={{0,2},{1,3},{2,0},{3,1},{4,6},{5,7},{6,4},{7,5},{8,10},{9,11},{10,... | collective-permute-start | bytes 1572872 | tf_op jit(solution)/shard_map/while/body/eval_jaxpr/ppermute | solution.py:31
  500.0 14.7 %collective-permute-start.3 = (f32[128,1024]{1,0:T(8,128)S(1)}, f32[128,1024]{1,0:T(8,128)S(1)}, u32[]{:S(2)}, u32[]{:S(2)}) collective-permute-start(f32[128,1024]{1,0:T(8,128)S(1)} %add.109), channel_id=1, source_target_pairs={{0,8},{1,9},{2,10},{3,11},{4,12},{5,13},{6,14},{7,15},{8,0},{9,1},... | collective-permute-start | bytes 1572872 | tf_op jit(solution)/shard_map/while/body/eval_jaxpr/ppermute | solution.py:31
  514.8 22.4 %collective-permute-start.4 = (f32[128,1024]{1,0:T(8,128)S(1)}, f32[128,1024]{1,0:T(8,128)S(1)}, u32[]{:S(2)}, u32[]{:S(2)}) collective-permute-start(f32[128,1024]{1,0:T(8,128)S(1)} %add.110), channel_id=1, source_target_pairs={{0,16},{1,17},{2,18},{3,19},{4,20},{5,21},{6,22},{7,23},{8,24},{9,... | collective-permute-start | bytes 1572872 | tf_op jit(solution)/shard_map/while/body/eval_jaxpr/ppermute | solution.py:31
  546.0 41.3 %collective-permute-start.5 = (f32[2048,128]{0,1:T(8,128)S(1)}, f32[2048,128]{0,1:T(8,128)S(1)}, u32[]{:S(2)}, u32[]{:S(2)}) collective-permute-start(f32[2048,128]{0,1:T(8,128)S(1)} %fusion.21), channel_id=1, source_target_pairs={{0,32},{32,64},{64,96},{96,128},{128,160},{160,192},{192,224},{224... | collective-permute-start | bytes 3145736 | tf_op jit(solution)/shard_map/while/body/eval_jaxpr/ppermute | solution.py:10
  590.2 13.9 %collective-permute-start = (f32[128,1024]{1,0:T(8,128)S(1)}, f32[128,1024]{1,0:T(8,128)S(1)}, u32[]{:S(2)}, u32[]{:S(2)}) collective-permute-start(f32[128,1024]{1,0:T(8,128)S(1)} %fusion.20), channel_id=1, source_target_pairs={{0,1},{1,0},{2,3},{3,2},{4,5},{5,4},{6,7},{7,6},{8,9},{9,8},{10,11... | collective-permute-start | bytes 1572872 | tf_op jit(solution)/shard_map/while/body/eval_jaxpr/ppermute | solution.py:31
  604.2 14.7 %collective-permute-start.1 = (f32[128,1024]{1,0:T(8,128)S(1)}, f32[128,1024]{1,0:T(8,128)S(1)}, u32[]{:S(2)}, u32[]{:S(2)}) collective-permute-start(f32[128,1024]{1,0:T(8,128)S(1)} %add.107), channel_id=1, source_target_pairs={{0,2},{1,3},{2,0},{3,1},{4,6},{5,7},{6,4},{7,5},{8,10},{9,11},{10,... | collective-permute-start | bytes 1572872 | tf_op jit(solution)/shard_map/while/body/eval_jaxpr/ppermute | solution.py:31
  619.0 12.3 %collective-permute-start.2 = (f32[128,1024]{1,0:T(8,128)S(1)}, f32[128,1024]{1,0:T(8,128)S(1)}, u32[]{:S(2)}, u32[]{:S(2)}) collective-permute-start(f32[128,1024]{1,0:T(8,128)S(1)} %add.108), channel_id=1, source_target_pairs={{0,4},{1,5},{2,6},{3,7},{4,0},{5,1},{6,2},{7,3},{8,12},{9,13},{10,... | collective-permute-start | bytes 1572872 | tf_op jit(solution)/shard_map/while/body/eval_jaxpr/ppermute | solution.py:31
  631.3 25.5 %collective-permute-start.3 = (f32[128,1024]{1,0:T(8,128)S(1)}, f32[128,1024]{1,0:T(8,128)S(1)}, u32[]{:S(2)}, u32[]{:S(2)}) collective-permute-start(f32[128,1024]{1,0:T(8,128)S(1)} %add.109), channel_id=1, source_target_pairs={{0,8},{1,9},{2,10},{3,11},{4,12},{5,13},{6,14},{7,15},{8,0},{9,1},... | collective-permute-start | bytes 1572872 | tf_op jit(solution)/shard_map/while/body/eval_jaxpr/ppermute | solution.py:31
  656.9 28.9 %collective-permute-start.4 = (f32[128,1024]{1,0:T(8,128)S(1)}, f32[128,1024]{1,0:T(8,128)S(1)}, u32[]{:S(2)}, u32[]{:S(2)}) collective-permute-start(f32[128,1024]{1,0:T(8,128)S(1)} %add.110), channel_id=1, source_target_pairs={{0,16},{1,17},{2,18},{3,19},{4,20},{5,21},{6,22},{7,23},{8,24},{9,... | collective-permute-start | bytes 1572872 | tf_op jit(solution)/shard_map/while/body/eval_jaxpr/ppermute | solution.py:31
  718.6 15.8 %collective-permute-start.1 = (f32[128,1024]{1,0:T(8,128)S(1)}, f32[128,1024]{1,0:T(8,128)S(1)}, u32[]{:S(2)}, u32[]{:S(2)}) collective-permute-start(f32[128,1024]{1,0:T(8,128)S(1)} %add.107), channel_id=1, source_target_pairs={{0,2},{1,3},{2,0},{3,1},{4,6},{5,7},{6,4},{7,5},{8,10},{9,11},{10,... | collective-permute-start | bytes 1572872 | tf_op jit(solution)/shard_map/while/body/eval_jaxpr/ppermute | solution.py:31
  744.3 48.7 %collective-permute-start.3 = (f32[128,1024]{1,0:T(8,128)S(1)}, f32[128,1024]{1,0:T(8,128)S(1)}, u32[]{:S(2)}, u32[]{:S(2)}) collective-permute-start(f32[128,1024]{1,0:T(8,128)S(1)} %add.109), channel_id=1, source_target_pairs={{0,8},{1,9},{2,10},{3,11},{4,12},{5,13},{6,14},{7,15},{8,0},{9,1},... | collective-permute-start | bytes 1572872 | tf_op jit(solution)/shard_map/while/body/eval_jaxpr/ppermute | solution.py:31
  793.1 25.5 %collective-permute-start.4 = (f32[128,1024]{1,0:T(8,128)S(1)}, f32[128,1024]{1,0:T(8,128)S(1)}, u32[]{:S(2)}, u32[]{:S(2)}) collective-permute-start(f32[128,1024]{1,0:T(8,128)S(1)} %add.110), channel_id=1, source_target_pairs={{0,16},{1,17},{2,18},{3,19},{4,20},{5,21},{6,22},{7,23},{8,24},{9,... | collective-permute-start | bytes 1572872 | tf_op jit(solution)/shard_map/while/body/eval_jaxpr/ppermute | solution.py:31
  850.1 12.1 %collective-permute-start.1 = (f32[128,1024]{1,0:T(8,128)S(1)}, f32[128,1024]{1,0:T(8,128)S(1)}, u32[]{:S(2)}, u32[]{:S(2)}) collective-permute-start(f32[128,1024]{1,0:T(8,128)S(1)} %add.107), channel_id=1, source_target_pairs={{0,2},{1,3},{2,0},{3,1},{4,6},{5,7},{6,4},{7,5},{8,10},{9,11},{10,... | collective-permute-start | bytes 1572872 | tf_op jit(solution)/shard_map/while/body/eval_jaxpr/ppermute | solution.py:31
  870.5 15.0 %collective-permute-start.3 = (f32[128,1024]{1,0:T(8,128)S(1)}, f32[128,1024]{1,0:T(8,128)S(1)}, u32[]{:S(2)}, u32[]{:S(2)}) collective-permute-start(f32[128,1024]{1,0:T(8,128)S(1)} %add.109), channel_id=1, source_target_pairs={{0,8},{1,9},{2,10},{3,11},{4,12},{5,13},{6,14},{7,15},{8,0},{9,1},... | collective-permute-start | bytes 1572872 | tf_op jit(solution)/shard_map/while/body/eval_jaxpr/ppermute | solution.py:31
  885.5 16.7 %collective-permute-start.4 = (f32[128,1024]{1,0:T(8,128)S(1)}, f32[128,1024]{1,0:T(8,128)S(1)}, u32[]{:S(2)}, u32[]{:S(2)}) collective-permute-start(f32[128,1024]{1,0:T(8,128)S(1)} %add.110), channel_id=1, source_target_pairs={{0,16},{1,17},{2,18},{3,19},{4,20},{5,21},{6,22},{7,23},{8,24},{9,... | collective-permute-start | bytes 1572872 | tf_op jit(solution)/shard_map/while/body/eval_jaxpr/ppermute | solution.py:31
  911.0 32.7 %collective-permute-start.5 = (f32[2048,128]{0,1:T(8,128)S(1)}, f32[2048,128]{0,1:T(8,128)S(1)}, u32[]{:S(2)}, u32[]{:S(2)}) collective-permute-start(f32[2048,128]{0,1:T(8,128)S(1)} %fusion.21), channel_id=1, source_target_pairs={{0,32},{32,64},{64,96},{96,128},{128,160},{160,192},{192,224},{224... | collective-permute-start | bytes 3145736 | tf_op jit(solution)/shard_map/while/body/eval_jaxpr/ppermute | solution.py:10
  (24 other events, 396.0 us)
